TPU v7x, 128 devices: a whole 4x4x4 slice. The times are simulated.
128 devices in a mesh: front: 8 (over x, core), wide: 16 (over z, y).
Axes of the slice: x: 4, y: 4, z: 4, core: 2. Of those that a mesh axis runs over, the one named last changes fastest.
Arguments:
- inv_diag: bfloat16 [8, 8192, 8192], P('front', 'wide'), as said below
- below: bfloat16 [8, 12288, 8192], P('front', 'wide'), may hold values from -0.0625 to 0.0625
- rhs: bfloat16 [8, 8192, 256], P('front', 'wide'), may hold values from -6 to 6
- tile_count: int32 [8], replicated, may hold values from 72 to 96, as said below
- tile_owner: int32 [8, 96, 1], P('front', 'wide'), may hold values from 0 to 7; in each aligned block of 6 rows (0 to 5, 6 to 11, ..., all dimensions but the last counted through in order) at most 2 rows name the same one
- tile_rows: int32 [8, 96, 128], P('front', 'wide'), may hold values from 0 to 511
- parent_rhs: bfloat16 [8, 8192, 256], P('front', 'wide'), may hold values from -6 to 6
Outputs:
- solved: bfloat16 [8, 8192, 256], P('front', 'wide')
- parent_new: float32 [8, 8192, 256], P('front', 'wide')
Inputs may be any that keep to these rules, and one draw needn't show every extreme that they name: Each inv_diag[f] is lower triangular. Tiles of front f with index at least tile_count[f] carry nothing; some front has all 96 tiles live. `tile_owner`: among the 6 tiles of one device (aligned blocks of tiles), no front index is named more than 2 times.
All inputs are finite; a program needn't handle non-finite values.
Results may differ from a plain program's by a relative error of at most 0.0037.
Values may be sent and summed in bfloat16 or wider, within the bound.
A program may use at most 128 MiB of HBM per device.

v0:
```python
import jax
import jax.numpy as jnp
from jax import lax
from jax.sharding import PartitionSpec as P

CAPACITY = 2


def body(inv_diag, below, rhs, tile_count, tile_owner, tile_rows, parent_rhs):
    inv_rows = inv_diag[0]
    below_rows = below[0]
    rhs_rows = rhs[0]
    rhs_width = rhs_rows.shape[1]
    gathered = lax.all_gather(rhs_rows, "wide", axis=0, tiled=True)
    solved = jnp.dot(inv_rows, gathered, preferred_element_type=jnp.float32).astype(jnp.bfloat16)
    solved_all = lax.all_gather(solved, "wide", axis=0, tiled=True)
    update_rows = jnp.dot(below_rows, solved_all, preferred_element_type=jnp.float32)
    tiles_here = tile_owner.shape[1]
    tile_height = tile_rows.shape[2]
    parent_height = parent_rhs.shape[1]
    group_index = lax.axis_index("front")
    wide_index = lax.axis_index("wide")
    count_live = lax.dynamic_index_in_dim(tile_count, group_index, 0, keepdims=False)
    numbers = wide_index * tiles_here + jnp.arange(tiles_here, dtype=jnp.int32)
    alive = numbers < count_live
    update_tiles = update_rows.astype(jnp.bfloat16).reshape(tiles_here, tile_height, rhs_width)
    update_tiles = jnp.where(alive[:, None, None], update_tiles, jnp.zeros_like(update_tiles))
    targets = jnp.where(alive[:, None], tile_rows[0], parent_height)
    owners = tile_owner[0, :, 0]
    front_count = lax.axis_size("front")
    slot_count = CAPACITY
    serial = jnp.arange(tiles_here, dtype=jnp.int32)
    same_owner = owners[:, None] == owners[None, :]
    earlier = serial[None, :] < serial[:, None]
    slot_index = jnp.sum((same_owner & earlier).astype(jnp.int32), axis=1)
    slot_place = owners * slot_count + slot_index
    chooser = jnp.arange(front_count * slot_count, dtype=jnp.int32)[:, None] == slot_place[None, :]
    tile_values = jnp.dot(
        chooser.astype(jnp.bfloat16),
        update_tiles.reshape(tiles_here, tile_height * rhs_width),
        preferred_element_type=jnp.float32,
    )
    tile_values = tile_values.astype(jnp.bfloat16).reshape(
        front_count, slot_count, tile_height, rhs_width
    )
    occupied = jnp.any(chooser, axis=1)
    picked_rows = jnp.sum(chooser.astype(jnp.int32)[:, :, None] * targets[None, :, :], axis=1)
    rows_sent = jnp.where(occupied[:, None], picked_rows, parent_height)
    rows_sent = rows_sent.reshape(front_count, slot_count, tile_height)
    arrived_values, arrived_rows = (
        lax.all_to_all(tile_values, "front", split_axis=0, concat_axis=0, tiled=True),
        lax.all_to_all(rows_sent, "front", split_axis=0, concat_axis=0, tiled=True),
    )
    flat_values = arrived_values.reshape(-1, rhs_width)
    flat_rows = arrived_rows.reshape(-1)
    placement_hits = (
        jnp.arange(parent_height, dtype=jnp.int32)[:, None] == flat_rows[None, :]
    ).astype(jnp.bfloat16)
    incoming = jnp.dot(placement_hits, flat_values, preferred_element_type=jnp.float32)
    parent_new = parent_rhs[0].astype(jnp.float32) - incoming
    return (solved[None], parent_new[None])


def solution(mesh):
    return jax.shard_map(
        body,
        mesh=mesh,
        in_specs=(
            P("front", "wide", None),
            P("front", "wide", None),
            P("front", "wide", None),
            P(),
            P("front", "wide", None),
            P("front", "wide", None),
            P("front", "wide", None),
        ),
        out_specs=(P("front", "wide", None), P("front", "wide", None)),
        check_vma=False,
    )
```

profile of v0, /device:TPU:1, one launch (start us, length us, event | category | flops | bytes accessed | tf_op | source)
XLA Modules:
  0.0 162.7 jit_solution(9237528288694343776)
XLA Ops:
  7.2 0.0 all-gather.6.cloned.1.call-start
  7.2 0.7 all-gather.6.cloned.1.call-update
  7.9 0.0 copy-start.2
  7.9 0.0 copy-start
  7.9 0.0 copy-start.3
  7.9 0.0 all-gather.4.cloned.1.call-start
  8.0 56.7 %all-gather.6.cloned.1.call-done = bf16[1,8192,256]{2,1,0:T(8,128)(2,1)} async-done(((bf16[1,512,256]{2,1,0:T(8,128)(2,1)}), bf16[1,8192,256]{2,1,0:T(8,128)(2,1)}) %all-gather.6.cloned.1.call-update) | async-done | bytes 4194320 | tf_op jit(solution)/shard_map/all_gather | solution.py:14
  64.7 7.6 %fusion.15 = bf16[512,256]{1,0:T(8,128)(2,1)} fusion(bf16[1,8192,256]{2,1,0:T(8,128)(2,1)} %all-gather.6.cloned.1.call-done, bf16[1,512,8192]{2,1,0:T(8,128)(2,1)} %param.7), kind=kOutput, calls=%fused_computation.13 | convolution fusion | flops 2147614720 | bytes 12845056 | tf_op jit(solution)/shard_map/dot_general | solution.py:15
  72.3 0.0 all-gather.4.cloned.1.call-update
  72.4 0.0 copy-done.2
  72.4 0.6 dynamic_slice.4
  73.0 0.7 add_compare_fusion
  73.6 0.0 copy-done
  73.6 0.1 broadcast_select_fusion.1
  73.7 0.0 copy-done.3
  73.7 0.2 convert_reduce_fusion
  73.9 0.1 fusion.24
  74.0 0.1 broadcast_in_dim.54
  74.1 0.1 multiply_reduce_fusion
  74.2 0.7 broadcast_select_fusion
  74.9 5.1 %all-to-all-start = ((s32[8,2,128]{2,1,0:T(2,128)}), s32[8,2,128]{2,1,0:T(2,128)S(1)}, u32[]{:S(2)}, u32[]{:S(2)}) async-start(s32[8,2,128]{2,1,0:T(2,128)} %broadcast_select_fusion), calls=%async_computation | async-start | bytes 16384 | tf_op jit(solution)/shard_map/all_to_all | solution.py:52
  79.9 43.7 %all-gather.4.cloned.1.call-done = bf16[8192,256]{1,0:T(8,128)(2,1)} async-done(((bf16[512,256]{1,0:T(8,128)(2,1)}), bf16[8192,256]{1,0:T(8,128)(2,1)}) %all-gather.4.cloned.1.call-update) | async-done | bytes 4194320 | tf_op jit(solution)/shard_map/all_gather | solution.py:16
  123.6 9.3 %fusion.12 = bf16[768,256]{0,1:T(8,128)(2,1)S(1)} fusion(bf16[8192,256]{1,0:T(8,128)(2,1)} %all-gather.4.cloned.1.call-done, bf16[1,768,8192]{2,1,0:T(8,128)(2,1)} %param.8), kind=kOutput, calls=%fused_computation.12 | convolution fusion | flops 3221422080 | bytes 17170432 | tf_op jit(solution)/shard_map/dot_general | solution.py:17
  133.0 0.0 copy-start.1
  133.0 0.2 copy.10
  133.1 0.4 reshape.73
  133.6 0.6 convolution_convert_fusion
  134.2 0.2 copy.12
  134.4 0.0 all-to-all-done
  134.4 19.8 %all_to_all.10 = bf16[8,2,128,256]{3,2,1,0:T(8,128)(2,1)S(1)} all-to-all(bf16[8,2,128,256]{3,2,1,0:T(8,128)(2,1)S(1)} %bitcast.39), channel_id=1, replica_groups=mesh['front'=8,'wide'=16] {'front'}, dimensions={0} | all-to-all | bytes 2097152 | tf_op jit(solution)/shard_map/all_to_all | solution.py:51
  154.2 0.0 copy-done.1
  154.3 1.6 fusion.11
  (2 shorter events, 0.0 us)
Async XLA Ops:
  7.2 57.5 %all-gather.6.cloned.1.call-start = ((), (), s32[]{:S(2)}) async-start(), calls=%async_computation.3 | async-start | bytes 4456448 | tf_op jit(solution)/shard_map/all_gather | solution.py:14
  7.9 64.5 %copy-start.2 = (s32[8]{0:T(128)S(1)}, s32[8]{0:T(128)}, u32[]{:S(2)}) copy-start(s32[8]{0:T(128)} %param.10) | copy-start | bytes 100
  7.9 65.7 %copy-start = (s32[1,6,128]{2,0,1:T(1,128)S(1)}, s32[1,6,128]{2,0,1:T(1,128)}, u32[]{:S(2)}) copy-start(s32[1,6,128]{2,0,1:T(1,128)} %param.12) | copy-start | bytes 9220
  7.9 65.8 %copy-start.3 = (s32[1,6,1]{1,2,0:T(1,128)S(1)}, s32[1,6,1]{1,2,0:T(1,128)}, u32[]{:S(2)}) copy-start(s32[1,6,1]{1,2,0:T(1,128)} %param.11) | copy-start | bytes 76
  7.9 115.7 %all-gather.4.cloned.1.call-start = ((), (), s32[]{:S(2)}) async-start(), calls=%async_computation.2 | async-start | bytes 4456448 | tf_op jit(solution)/shard_map/all_gather | solution.py:16
  74.9 59.6 %all-to-all-start = ((s32[8,2,128]{2,1,0:T(2,128)}), s32[8,2,128]{2,1,0:T(2,128)S(1)}, u32[]{:S(2)}, u32[]{:S(2)}) async-start(s32[8,2,128]{2,1,0:T(2,128)} %broadcast_select_fusion), calls=%async_computation | async-start | bytes 16384 | tf_op jit(solution)/shard_map/all_to_all | solution.py:52
  133.0 21.3 %copy-start.1 = (bf16[1,512,256]{2,1,0:T(8,128)(2,1)S(1)}, bf16[1,512,256]{2,1,0:T(8,128)(2,1)}, u32[]{:S(2)}) copy-start(bf16[1,512,256]{2,1,0:T(8,128)(2,1)} %param.13) | copy-start | bytes 786436
Sparse Core Ops, SparseCore 0:
  10.1 54.5 all-gather.5
  72.5 51.0 all-gather.3
where the time goes:
time: 163 us
  waiting for transfers between devices  101 us (62%)
  blocking collectives  19.8 us (12%)
  matrix products  19.1 us (12%)
  between operations  14.2 us (9%)
  starting transfers between devices  5.17 us (3%)
  other arithmetic  1.76 us (1%)
    all_gather x1, waiting for transfers between devices, body(): gathered = lax.all_gather(rhs_rows, 'wide', axis=0, tiled=True)  56.7 us
    all_gather x1, waiting for transfers between devices, body(): solved_all = lax.all_gather(solved, 'wide', axis=0, tiled=True)  43.7 us
    all_to_all x1, blocking collectives, body(): lax.all_to_all(tile_values, 'front', split_axis=0, concat_axis=0, tiled=T...  19.8 us
    dot_general x1, matrix products, body(): jnp.dot(below_rows, solved_all, preferred_element_type=jnp.float32)  9.32 us
    dot_general x1, matrix products, body(): jnp.dot(inv_rows, gathered, preferred_element_type=jnp.float32)  7.65 us
    all_to_all x1, starting transfers between devices, body(): lax.all_to_all(rows_sent, 'front', split_axis=0, concat_axis=0, tiled=True)  5.09 us
  transfers between devices with their start and end apart: 3, of which 2 were waited for; matrix products, arithmetic and copies ran while one was open for 8% of the time, Pallas kernels for 0%

commit v1 on v0

v1 whole, which is shorter than its diff:
```python
import functools

import jax
import jax.numpy as jnp
from jax import lax
from jax.experimental import pallas as pl
from jax.experimental.pallas import tpu as pltpu
from jax.sharding import PartitionSpec as P

MESH = pl.DeviceIdType.MESH
CHUNK = 128
PLUS, MINUS = 1, -1
DIRS = [(a, s) for a in (0, 1) for s in (PLUS, MINUS)]
D1, R1, OWN, NEAR_M, NEAR_P, OPP_A, OPP_B, R_OWN, R_NEAR_M, R_NEAR_P, R_OPP = range(11)
PER_LINK = 11


def kernel(
    inv_hbm, below_hbm, rhs_hbm, parent_hbm, rows_ref, owner_ref, count_ref,
    solved_hbm, parent_out_hbm,
    inv, below, rbuf, sbuf, s_acc, u_acc, u_tiles, slot_idx,
    rows_out, rows_in, packed, arrived, relayed, hits, parent, parent_out,
    g_send, g_recv, x_send, x_recv, r_send, r_recv, loc, out_sem,
):
    f = lax.axis_index("front")
    w = lax.axis_index("wide")
    z, y = w // 4, w % 4
    chip, core = f // 2, f % 2
    pb = rbuf.shape[1] // 16
    half, quarter = pb // 2, pb // 4
    tiles, height = u_tiles.shape[0], u_tiles.shape[1]
    slots = arrived.shape[2]
    parent_rows = parent.shape[0]
    chunks = rbuf.shape[0]
    bufs = [rbuf.at[c] for c in range(chunks)] + [sbuf.at[c] for c in range(chunks)]
    sends = []

    def wide_of(off):
        return ((z + off[1] + 4) % 4) * 4 + (y + off[0] + 4) % 4

    def vec(axis, k):
        return (k, 0) if axis == 0 else (0, k)

    def add(p, q):
        return (p[0] + q[0], p[1] + q[1])

    def region(g, off, h, q=None):
        start = wide_of(off) * pb + h * half + (0 if q is None else q * quarter)
        size = half if q is None else quarter
        return bufs[g].at[pl.ds(pl.multiple_of(start, quarter), size)]

    def gcopy(g, axis, s, msg, ref):
        i = (axis * 2 + (0 if s == PLUS else 1)) * PER_LINK + msg
        return pltpu.make_async_remote_copy(
            src_ref=ref, dst_ref=ref, send_sem=g_send.at[g, i], recv_sem=g_recv.at[g, i],
            device_id=(f, wide_of(vec(axis, s))), device_id_type=MESH,
        )

    def gsend(g, axis, s, msg, ref):
        copy = gcopy(g, axis, s, msg, ref)
        copy.start()
        sends.append(copy)

    def gwait(g, axis, s, msg, ref):
        gcopy(g, axis, s, msg, ref).wait_recv()

    def quart(s):
        return 0 if s == PLUS else 1

    here = (0, 0)

    def g_own(g):
        for axis, s in DIRS:
            gsend(g, axis, s, D1, region(g, here, axis))
        for axis, s in DIRS:
            gsend(g, axis, s, OWN, region(g, here, 1 - axis))

    def g_d1(g):
        for axis, s in DIRS:
            off = vec(axis, -s)
            gwait(g, axis, s, D1, region(g, off, axis))
            gsend(g, axis, s, R1, region(g, off, axis, quart(s)))
            for t in (PLUS, MINUS):
                gsend(g, 1 - axis, t, NEAR_M if s == PLUS else NEAR_P, region(g, off, axis))

    def g_r1(g):
        for axis, s in DIRS:
            ref = region(g, vec(axis, 2), axis, quart(s))
            gwait(g, axis, s, R1, ref)
            for t in (PLUS, MINUS):
                gsend(g, 1 - axis, t, OPP_A if s == PLUS else OPP_B, ref)

    def g_d2own(g):
        for axis, s in DIRS:
            off = vec(axis, -s)
            gwait(g, axis, s, OWN, region(g, off, 1 - axis))
            gsend(g, axis, s, R_OWN, region(g, off, 1 - axis, quart(s)))

    def g_d2near(g):
        for j, msg, relay in ((MINUS, NEAR_M, R_NEAR_M), (PLUS, NEAR_P, R_NEAR_P)):
            for axis, s in DIRS:
                off = add(vec(axis, -s), vec(1 - axis, j))
                gwait(g, axis, s, msg, region(g, off, 1 - axis))
                gsend(g, axis, s, relay, region(g, off, 1 - axis, quart(s)))

    def g_d2opp(g):
        for axis, s in DIRS:
            off = add(vec(axis, -s), vec(1 - axis, 2))
            for q, msg in ((0, OPP_A), (1, OPP_B)):
                ref = region(g, off, 1 - axis, q)
                gwait(g, axis, s, msg, ref)
                if q == quart(s):
                    gsend(g, axis, s, R_OPP, ref)

    def g_r2(g, msg, j):
        for axis, s in DIRS:
            off = add(vec(axis, 2), vec(1 - axis, j))
            gwait(g, axis, s, msg, region(g, off, 1 - axis, quart(s)))

    def g_r2all(g):
        for msg, j in ((R_OWN, 0), (R_NEAR_M, MINUS), (R_NEAR_P, PLUS), (R_OPP, 2)):
            g_r2(g, msg, j)

    own = pl.ds(pl.multiple_of(w * pb, pb), pb)
    loads = []
    for c in range(chunks):
        cols = pl.ds(c * CHUNK, CHUNK)
        loads.append(pltpu.make_async_copy(rhs_hbm.at[:, cols], rbuf.at[c, own], loc.at[c]))
    loads.append(pltpu.make_async_copy(inv_hbm, inv, loc.at[chunks]))
    loads.append(pltpu.make_async_copy(below_hbm, below, loc.at[chunks + 1]))
    loads.append(pltpu.make_async_copy(parent_hbm, parent, loc.at[chunks + 2]))
    for copy in loads:
        copy.start()

    barrier = pltpu.get_barrier_semaphore()
    for axis, s in DIRS:
        pl.semaphore_signal(barrier, inc=1, device_id=(f, wide_of(vec(axis, s))), device_id_type=MESH)
    for d in range(1, 8):
        pl.semaphore_signal(barrier, inc=1, device_id=((f + d) % 8, w), device_id_type=MESH)
    pl.semaphore_wait(barrier, 11)

    loads[0].wait()
    g_own(0)

    live = [w * tiles + j < count_ref[f] for j in range(tiles)]
    none = jnp.full((1, height), parent_rows, jnp.int32)
    rows_out[...] = jnp.full(rows_out.shape, parent_rows, jnp.int32)
    for g in range(8):
        index = [jnp.int32(0)] * slots
        found = [jnp.int32(0)] * slots
        seen = jnp.int32(0)
        for j in range(tiles):
            hit = owner_ref[j] == g
            for k in range(slots):
                this = jnp.logical_and(hit, seen == k)
                index[k] = jnp.where(this, j, index[k])
                found[k] = jnp.where(jnp.logical_and(this, live[j]), 1, found[k])
            seen = seen + jnp.where(hit, 1, 0)
        for k in range(slots):
            slot_idx[g * slots + k] = index[k]
            rows_out[g, k:k + 1, :] = jnp.where(found[k] == 1, rows_ref[pl.ds(index[k], 1), :], none)
    rows_in[f] = rows_out[f]
    rcopies = []
    for d in range(1, 8):
        to = (f + d) % 8
        copy = pltpu.make_async_remote_copy(
            src_ref=rows_out.at[to], dst_ref=rows_in.at[f], send_sem=r_send.at[d], recv_sem=r_recv.at[d],
            device_id=(to, w), device_id_type=MESH,
        )
        copy.start()
        sends.append(copy)

    def wait_rows():
        for d in range(1, 8):
            pltpu.make_async_remote_copy(
                src_ref=rows_in.at[(f + 8 - d) % 8], dst_ref=rows_in.at[(f + 8 - d) % 8],
                send_sem=r_send.at[d], recv_sem=r_recv.at[d], device_id=((f + d) % 8, w), device_id_type=MESH,
            ).wait_recv()

    def build_hits():
        position = lax.broadcasted_iota(jnp.int32, (parent_rows, height), 0)

        def one(i, carry):
            for k in range(slots):
                row = rows_in[i, k:k + 1, :]
                at = pl.ds(pl.multiple_of((i * slots + k) * height, height), height)
                hits[:, at] = jnp.where(position == row, 1.0, 0.0).astype(jnp.bfloat16)
            return carry

        lax.fori_loop(0, 8, one, 0)

    def block(ref, acc, src, k):
        at = pl.ds(pl.multiple_of(k * pb, pb), pb)
        acc[...] += jnp.dot(ref[:, at], src[at, :], preferred_element_type=jnp.float32)

    def mm(ref, acc, src, lo, hi, place=lambda i: i):
        def step(i, carry):
            block(ref, acc, src, place(i))
            return carry

        lax.fori_loop(lo, hi, step, 0)

    def store_solved(c):
        sbuf[c, own, :] = s_acc[...].astype(jnp.bfloat16)

    def solved_out(c):
        copy = pltpu.make_async_copy(sbuf.at[c, own], solved_hbm.at[:, pl.ds(c * CHUNK, CHUNK)], out_sem.at[c])
        copy.start()
        return copy

    def xcopy(c, sid, rid, src, dst, to):
        return pltpu.make_async_remote_copy(
            src_ref=src, dst_ref=dst, send_sem=x_send.at[c, sid], recv_sem=x_recv.at[c, rid],
            device_id=(to, w), device_id_type=MESH,
        )

    def xstart(*args):
        copy = xcopy(*args)
        copy.start()
        sends.append(copy)

    def chip_at(k):
        return (chip + k + 4) % 4

    def pack(c):
        for j in range(tiles):
            value = u_acc[j * height:(j + 1) * height, :]
            u_tiles[j] = jnp.where(live[j], value, jnp.zeros_like(value)).astype(jnp.bfloat16)

        def one(i, carry):
            for k in range(slots):
                packed[c, i, k] = u_tiles[slot_idx[i * slots + k]]
            return carry

        lax.fori_loop(0, 8, one, 0)
        for k in range(slots):
            arrived[c, f, k] = packed[c, f, k]

    def xsend(c):
        for n, s in enumerate((PLUS, MINUS)):
            for c2 in range(2):
                to = chip_at(2) * 2 + c2
                xstart(c, 5 + n * 2 + c2, 5 + n * 2 + c2, packed.at[c, to, n], relayed.at[c, n, c2], chip_at(s) * 2 + core)
        for n, s in enumerate((PLUS, MINUS)):
            for c2 in range(2):
                to = chip_at(s) * 2 + c2
                xstart(c, 1 + n * 2 + c2, 1 + n * 2 + core, packed.at[c, to], arrived.at[c, f], to)
        to = chip * 2 + 1 - core
        xstart(c, 0, 0, packed.at[c, to], arrived.at[c, f], to)

    def xrelay(c):
        for n, s in enumerate((PLUS, MINUS)):
            for c2 in range(2):
                ref = relayed.at[c, n, c2]
                xcopy(c, 5 + n * 2 + c2, 5 + n * 2 + c2, ref, ref, chip_at(s) * 2 + core).wait_recv()
                source = chip_at(-s) * 2 + core
                xstart(c, 9 + n * 2 + c2, 9 + n * 2 + core, ref, arrived.at[c, source, n], chip_at(s) * 2 + c2)

    def xwait(c):
        other = chip * 2 + 1 - core
        ref = arrived.at[c, other]
        xcopy(c, 0, 0, ref, ref, other).wait_recv()
        for n, s in enumerate((PLUS, MINUS)):
            for c2 in range(2):
                ref = arrived.at[c, chip_at(-s) * 2 + c2]
                xcopy(c, 0, 1 + n * 2 + c2, ref, ref, other).wait_recv()
        for n, s in enumerate((PLUS, MINUS)):
            for c2 in range(2):
                ref = arrived.at[c, chip_at(2) * 2 + c2, n]
                xcopy(c, 0, 9 + n * 2 + c2, ref, ref, other).wait_recv()

    def scatter(c):
        cols = slice(c * CHUNK, (c + 1) * CHUNK)
        per = 4 * slots * height

        def step(i, acc):
            at = pl.ds(pl.multiple_of(i * per, per), per)
            values = arrived[c, pl.ds(i * 4, 4)].reshape(per, CHUNK)
            return acc - jnp.dot(hits[:, at], values, preferred_element_type=jnp.float32)

        parent_out[c] = parent[:, cols].astype(jnp.float32)
        for i in range(2):
            parent_out[c] = step(i, parent_out[c])
        copy = pltpu.make_async_copy(parent_out.at[c], parent_out_hbm.at[:, pl.ds(c * CHUNK, CHUNK)], out_sem.at[chunks + c])
        copy.start()
        return copy

    nb = 16
    R, S = (0, 1), (2, 3)
    g_d1(0)
    g_r1(0)
    loads[1].wait()
    g_own(1)
    g_d2own(0)
    g_d2near(0)
    g_d2opp(0)
    g_d1(1)
    g_r2all(0)
    g_r1(1)
    loads[2].wait()
    s_acc[...] = jnp.zeros_like(s_acc)
    mm(inv, s_acc, rbuf.at[0], 0, 5)
    g_d2own(1)
    mm(inv, s_acc, rbuf.at[0], 5, 11)
    g_d2near(1)
    mm(inv, s_acc, rbuf.at[0], 11, nb)
    store_solved(0)
    g_own(2)
    g_d2opp(1)
    outs = [solved_out(0)]
    g_d1(2)
    g_r2all(1)
    g_r1(2)
    s_acc[...] = jnp.zeros_like(s_acc)
    mm(inv, s_acc, rbuf.at[1], 0, 5)
    g_d2own(2)
    mm(inv, s_acc, rbuf.at[1], 5, 11)
    g_d2near(2)
    mm(inv, s_acc, rbuf.at[1], 11, nb)
    store_solved(1)
    g_own(3)
    g_d2opp(2)
    outs.append(solved_out(1))
    wait_rows()
    g_d1(3)
    g_r2all(2)
    g_r1(3)
    loads[3].wait()
    u_acc[...] = jnp.zeros_like(u_acc)
    mm(below, u_acc, sbuf.at[0], 0, 5)
    g_d2own(3)
    mm(below, u_acc, sbuf.at[0], 5, 11)
    g_d2near(3)
    mm(below, u_acc, sbuf.at[0], 11, nb)
    pack(0)
    xsend(0)
    g_d2opp(3)
    u_acc[...] = jnp.zeros_like(u_acc)
    src = sbuf.at[1]
    mm(below, u_acc, src, 0, 1, lambda i: w)
    mm(below, u_acc, src, 0, 4, lambda i: wide_of(((2 * (i % 2) - 1) * (1 - i // 2), (2 * (i % 2) - 1) * (i // 2))))
    xrelay(0)
    mm(below, u_acc, src, 0, 4, lambda i: wide_of((2 * (i % 2) - 1, 2 * (i // 2) - 1)))
    build_hits()
    g_r2(3, R_OWN, 0)
    mm(below, u_acc, src, 0, 2, lambda i: wide_of((2 * i, 2 - 2 * i)))
    g_r2(3, R_NEAR_M, MINUS)
    g_r2(3, R_NEAR_P, PLUS)
    mm(below, u_acc, src, 0, 4, lambda i: wide_of((
        2 * (1 - i // 2) + (2 * (i % 2) - 1) * (i // 2), (2 * (i % 2) - 1) * (1 - i // 2) + 2 * (i // 2))))
    g_r2(3, R_OPP, 2)
    mm(below, u_acc, src, 0, 1, lambda i: wide_of((2, 2)))
    pack(1)
    xsend(1)
    xwait(0)
    loads[4].wait()
    outs.append(scatter(0))
    xrelay(1)
    xwait(1)
    outs.append(scatter(1))
    for copy in sends:
        copy.wait_send()
    for copy in outs:
        copy.wait()


def call(inv, below, rhs, parent_rhs, tile_rows, owners, tile_count):
    rows, pivots = inv.shape
    under = below.shape[0]
    width = rhs.shape[1]
    chunks = width // CHUNK
    tiles, height = tile_rows.shape
    slots = 2
    parent_rows = parent_rhs.shape[0]
    bf, f32 = jnp.bfloat16, jnp.float32
    anyspace = pl.BlockSpec(memory_space=pl.ANY)
    vmem = pl.BlockSpec(memory_space=pltpu.VMEM)
    smem = pl.BlockSpec(memory_space=pltpu.SMEM)
    dma = pltpu.SemaphoreType.DMA
    return pl.pallas_call(
        kernel,
        out_shape=(
            jax.ShapeDtypeStruct((rows, width), bf),
            jax.ShapeDtypeStruct((parent_rows, width), f32),
        ),
        in_specs=[anyspace] * 4 + [vmem, smem, smem],
        out_specs=(anyspace, anyspace),
        scratch_shapes=[
            pltpu.VMEM((rows, pivots), bf),
            pltpu.VMEM((under, pivots), bf),
            pltpu.VMEM((chunks, pivots, CHUNK), bf),
            pltpu.VMEM((chunks, pivots, CHUNK), bf),
            pltpu.VMEM((rows, CHUNK), f32),
            pltpu.VMEM((under, CHUNK), f32),
            pltpu.VMEM((tiles, height, CHUNK), bf),
            pltpu.SMEM((8 * slots,), jnp.int32),
            pltpu.VMEM((8, 8, height), jnp.int32),
            pltpu.VMEM((8, 8, height), jnp.int32),
            pltpu.VMEM((chunks, 8, slots, height, CHUNK), bf),
            pltpu.VMEM((chunks, 8, slots, height, CHUNK), bf),
            pltpu.VMEM((chunks, 2, 2, height, CHUNK), bf),
            pltpu.VMEM((parent_rows, 8 * slots * height), bf),
            pltpu.VMEM((parent_rows, width), bf),
            pltpu.VMEM((chunks, parent_rows, CHUNK), f32),
            dma((2 * chunks, 4 * PER_LINK)),
            dma((2 * chunks, 4 * PER_LINK)),
            dma((chunks, 13)),
            dma((chunks, 13)),
            dma((8,)),
            dma((8,)),
            dma((chunks + 3,)),
            dma((2 * chunks,)),
        ],
        compiler_params=pltpu.CompilerParams(
            collective_id=0, has_side_effects=True, vmem_limit_bytes=60 * 1024 * 1024
        ),
        name="solve_extend_add",
    )(inv, below, rhs, parent_rhs, tile_rows, owners, tile_count)


def body(inv_diag, below, rhs, tile_count, tile_owner, tile_rows, parent_rhs):
    solved, parent_new = call(
        inv_diag[0], below[0], rhs[0], parent_rhs[0], tile_rows[0], tile_owner[0, :, 0], tile_count
    )
    return solved[None], parent_new[None]


def solution(mesh):
    spec = P("front", "wide", None)
    return jax.shard_map(
        body,
        mesh=mesh,
        in_specs=(spec, spec, spec, P(), spec, spec, spec),
        out_specs=(spec, spec),
        check_vma=False,
    )
```

time: 163 us -> 89.3 us (0.55)
  waiting for transfers between devices: 101 us -> 0 us
  Pallas kernels: 0 us -> 83.6 us
  blocking collectives: 19.8 us -> 0 us
  matrix products: 19.1 us -> 0 us
  between operations: 14.2 us -> 0.64 us
  starting transfers between devices: 5.17 us -> 0 us
  local copies, waits for them, and re-layouts: 1.52 us -> 4.81 us
  other arithmetic: 1.76 us -> 0 us
    all_gather x2 -> x0, waiting for transfers between devices: 100 us -> none  [the longest x1 56.7 us: body(): gathered = lax.all_gather(rhs_rows, 'wide', axis=0, tiled=True)]
    pallas_call x0 -> x1, Pallas kernels: none -> 83.6 us  [call(): pl.pallas_call(kernel, out_shape=(jax.ShapeDtypeStruct((rows, width), bf)...]
    all_to_all x1 -> x0, blocking collectives: 19.8 us -> none  [body(): lax.all_to_all(tile_values, 'front', split_axis=0, concat_axis=0, tiled=T...]
    dot_general x4 -> x0, matrix products: 19.1 us -> none  [the longest x1 9.32 us: body(): jnp.dot(below_rows, solved_all, preferred_element_type=jnp.float32)]
    all_to_all x1 -> x0, starting transfers between devices: 5.09 us -> none  [body(): lax.all_to_all(rows_sent, 'front', split_axis=0, concat_axis=0, tiled=True)]
    unnamed x10 -> x3, local copies, waits for them, and re-layouts: 0.25 us -> 4.81 us
  transfers between devices with their start and end apart: 3 -> 0, of which waited for: 2 -> 0; matrix products, arithmetic and copies ran while one was open for 8% -> 0% of each run, Pallas kernels for 0% -> 0%
where the time goes in v1:
time: 89.3 us; the launch traced here: 89 us
  Pallas kernels  83.6 us (94%)
  local copies, waits for them, and re-layouts  4.81 us (5%)
    pallas_call x1, Pallas kernels, call(): pl.pallas_call(kernel, out_shape=(jax.ShapeDtypeStruct((rows, width), bf)...  83.6 us
    unnamed x3, local copies, waits for them, and re-layouts  4.81 us

profile of v1, /device:TPU:1, one launch (start us, length us, event | category | flops | bytes accessed | tf_op | source)
XLA Modules:
  0.0 89.0 jit_solution(2524761057474679641)
XLA Ops:
  0.6 1.3 %copy.11 = s32[1,6,128]{2,1,0:T(8,128)} copy(s32[1,6,128]{2,0,1:T(1,128)} %param.12) | data formatting | bytes 6144
  1.9 83.6 %solve_extend_add.1 = (bf16[512,256]{1,0:T(8,128)(2,1)}, f32[512,256]{1,0:T(8,128)}) custom-call(bf16[512,8192]{1,0:T(8,128)(2,1)} %bitcast.11, bf16[768,8192]{1,0:T(8,128)(2,1)} %bitcast.10, bf16[512,256]{1,0:T(8,128)(2,1)} %bitcast.13, bf16[512,256]{1,0:T(8,128)(2,1)} %bitcast.14, s32[6,128]{1,0:T(8,128)} %bitcast.16, s32[6]{0:T(128)} %bitcast.17, s32[8]{0:T(128)} %count_ref.1), custom_call_target="tpu_custom_call" | custom-call | tf_op jit(solution)/shard_map/solve_extend_add/pallas_call | solution.py:380
  85.5 1.7 %copy.14 = bf16[1,512,256]{2,1,0:T(8,128)(2,1)} copy(bf16[1,512,256]{2,1,0:T(8,128)(2,1)} %bitcast.15) | data formatting | bytes 524288
  87.2 1.9 %copy.15 = f32[1,512,256]{2,1,0:T(8,128)} copy(f32[1,512,256]{2,1,0:T(8,128)} %bitcast.12) | data formatting | bytes 1048576

commit v2 on v1

--- a/solution.py
+++ b/solution.py
@@ -17,10 +17,10 @@
 
 def kernel(
     inv_hbm, below_hbm, rhs_hbm, parent_hbm, rows_ref, owner_ref, count_ref,
-    solved_hbm, parent_out_hbm,
+    solved_out, parent_out,
     inv, below, rbuf, sbuf, s_acc, u_acc, u_tiles, slot_idx,
-    rows_out, rows_in, packed, arrived, relayed, hits, parent, parent_out,
-    g_send, g_recv, x_send, x_recv, r_send, r_recv, loc, out_sem,
+    rows_out, rows_in, packed, arrived, relayed, hits, parent,
+    g_send, g_recv, x_send, x_recv, r_send, r_recv, loc,
 ):
     f = lax.axis_index("front")
     w = lax.axis_index("wide")
@@ -158,7 +158,7 @@
             seen = seen + jnp.where(hit, 1, 0)
         for k in range(slots):
             slot_idx[g * slots + k] = index[k]
-            rows_out[g, k:k + 1, :] = jnp.where(found[k] == 1, rows_ref[pl.ds(index[k], 1), :], none)
+            rows_out[g, k:k + 1, :] = jnp.where(found[k] == 1, rows_ref[index[k]], none)
     rows_in[f] = rows_out[f]
     rcopies = []
     for d in range(1, 8):
@@ -199,14 +199,6 @@
             return carry
 
         lax.fori_loop(lo, hi, step, 0)
-
-    def store_solved(c):
-        sbuf[c, own, :] = s_acc[...].astype(jnp.bfloat16)
-
-    def solved_out(c):
-        copy = pltpu.make_async_copy(sbuf.at[c, own], solved_hbm.at[:, pl.ds(c * CHUNK, CHUNK)], out_sem.at[c])
-        copy.start()
-        return copy
 
     def xcopy(c, sid, rid, src, dst, to):
         return pltpu.make_async_remote_copy(
@@ -278,89 +270,116 @@
             values = arrived[c, pl.ds(i * 4, 4)].reshape(per, CHUNK)
             return acc - jnp.dot(hits[:, at], values, preferred_element_type=jnp.float32)
 
-        parent_out[c] = parent[:, cols].astype(jnp.float32)
-        for i in range(2):
-            parent_out[c] = step(i, parent_out[c])
-        copy = pltpu.make_async_copy(parent_out.at[c], parent_out_hbm.at[:, pl.ds(c * CHUNK, CHUNK)], out_sem.at[chunks + c])
-        copy.start()
-        return copy
-
-    nb = 16
-    R, S = (0, 1), (2, 3)
+        parent_out[:, cols] = step(1, step(0, parent[:, cols].astype(jnp.float32)))
+
+    def sign(i):
+        return 2 * (i % 2) - 1
+
+    def at_near(i):
+        return wide_of((sign(i) * (1 - i // 2), sign(i) * (i // 2)))
+
+    def at_diagonal(i):
+        return wide_of((sign(i), 2 * (i // 2) - 1))
+
+    def at_far(i):
+        return wide_of((2 * i, 2 - 2 * i))
+
+    def at_farther(i):
+        return wide_of((2 * (1 - i // 2) + sign(i) * (i // 2), sign(i) * (1 - i // 2) + 2 * (i // 2)))
+
+    sides = [(inv, s_acc)] * chunks + [(below, u_acc)] * chunks
+
+    def take(g, count, place):
+        mm(sides[g][0], sides[g][1], bufs[g], 0, count, place)
+
+    def take_own(g):
+        acc = sides[g][1]
+        acc[...] = jnp.zeros_like(acc)
+        take(g, 1, lambda i: w)
+
+    def middle(g):
+        take_own(g)
+        g_d2own(g)
+        take(g, 4, at_near)
+        g_d2near(g)
+
+    def late_first(g):
+        g_r2(g, R_OWN, 0)
+        take(g, 2, at_far)
+
+    def late_last(g):
+        g_r2(g, R_NEAR_M, MINUS)
+        g_r2(g, R_NEAR_P, PLUS)
+        take(g, 4, at_farther)
+        g_r2(g, R_OPP, 2)
+        take(g, 1, lambda i: wide_of((2, 2)))
+
+    def store_solved(c):
+        value = s_acc[...].astype(jnp.bfloat16)
+        sbuf[c, own, :] = value
+        solved_out[:, c * CHUNK:(c + 1) * CHUNK] = value
+
     g_d1(0)
     g_r1(0)
     loads[1].wait()
+    loads[2].wait()
+    middle(0)
     g_own(1)
-    g_d2own(0)
-    g_d2near(0)
+    take(0, 4, at_diagonal)
     g_d2opp(0)
+    wait_rows()
+    build_hits()
     g_d1(1)
-    g_r2all(0)
+    late_first(0)
     g_r1(1)
-    loads[2].wait()
-    s_acc[...] = jnp.zeros_like(s_acc)
-    mm(inv, s_acc, rbuf.at[0], 0, 5)
-    g_d2own(1)
-    mm(inv, s_acc, rbuf.at[0], 5, 11)
-    g_d2near(1)
-    mm(inv, s_acc, rbuf.at[0], 11, nb)
+    late_last(0)
     store_solved(0)
+    middle(1)
     g_own(2)
+    take(1, 4, at_diagonal)
     g_d2opp(1)
-    outs = [solved_out(0)]
     g_d1(2)
-    g_r2all(1)
+    late_first(1)
     g_r1(2)
-    s_acc[...] = jnp.zeros_like(s_acc)
-    mm(inv, s_acc, rbuf.at[1], 0, 5)
-    g_d2own(2)
-    mm(inv, s_acc, rbuf.at[1], 5, 11)
-    g_d2near(2)
-    mm(inv, s_acc, rbuf.at[1], 11, nb)
+    late_last(1)
     store_solved(1)
+    loads[3].wait()
+    middle(2)
     g_own(3)
+    take(2, 4, at_diagonal)
     g_d2opp(2)
-    outs.append(solved_out(1))
-    wait_rows()
     g_d1(3)
-    g_r2all(2)
+    late_first(2)
     g_r1(3)
-    loads[3].wait()
-    u_acc[...] = jnp.zeros_like(u_acc)
-    mm(below, u_acc, sbuf.at[0], 0, 5)
-    g_d2own(3)
-    mm(below, u_acc, sbuf.at[0], 5, 11)
-    g_d2near(3)
-    mm(below, u_acc, sbuf.at[0], 11, nb)
+    late_last(2)
     pack(0)
     xsend(0)
+    middle(3)
+    xrelay(0)
+    take(3, 4, at_diagonal)
     g_d2opp(3)
-    u_acc[...] = jnp.zeros_like(u_acc)
-    src = sbuf.at[1]
-    mm(below, u_acc, src, 0, 1, lambda i: w)
-    mm(below, u_acc, src, 0, 4, lambda i: wide_of(((2 * (i % 2) - 1) * (1 - i // 2), (2 * (i % 2) - 1) * (i // 2))))
-    xrelay(0)
-    mm(below, u_acc, src, 0, 4, lambda i: wide_of((2 * (i % 2) - 1, 2 * (i // 2) - 1)))
-    build_hits()
-    g_r2(3, R_OWN, 0)
-    mm(below, u_acc, src, 0, 2, lambda i: wide_of((2 * i, 2 - 2 * i)))
-    g_r2(3, R_NEAR_M, MINUS)
-    g_r2(3, R_NEAR_P, PLUS)
-    mm(below, u_acc, src, 0, 4, lambda i: wide_of((
-        2 * (1 - i // 2) + (2 * (i % 2) - 1) * (i // 2), (2 * (i % 2) - 1) * (1 - i // 2) + 2 * (i // 2))))
-    g_r2(3, R_OPP, 2)
-    mm(below, u_acc, src, 0, 1, lambda i: wide_of((2, 2)))
+    late_first(3)
+    late_last(3)
     pack(1)
     xsend(1)
+    loads[4].wait()
     xwait(0)
-    loads[4].wait()
-    outs.append(scatter(0))
+    scatter(0)
     xrelay(1)
     xwait(1)
-    outs.append(scatter(1))
+    scatter(1)
     for copy in sends:
         copy.wait_send()
-    for copy in outs:
+
+
+def write_kernel(solved_in, parent_in, solved_hbm, parent_hbm, sem):
+    copies = [
+        pltpu.make_async_copy(solved_in, solved_hbm, sem.at[0]),
+        pltpu.make_async_copy(parent_in, parent_hbm, sem.at[1]),
+    ]
+    for copy in copies:
+        copy.start()
+    for copy in copies:
         copy.wait()
 
 
@@ -369,22 +388,23 @@
     under = below.shape[0]
     width = rhs.shape[1]
     chunks = width // CHUNK
-    tiles, height = tile_rows.shape
+    tiles, _, height = tile_rows.shape
     slots = 2
     parent_rows = parent_rhs.shape[0]
     bf, f32 = jnp.bfloat16, jnp.float32
     anyspace = pl.BlockSpec(memory_space=pl.ANY)
+    hbm = pl.BlockSpec(memory_space=pltpu.HBM)
     vmem = pl.BlockSpec(memory_space=pltpu.VMEM)
     smem = pl.BlockSpec(memory_space=pltpu.SMEM)
     dma = pltpu.SemaphoreType.DMA
-    return pl.pallas_call(
+    solved, parent_new = pl.pallas_call(
         kernel,
         out_shape=(
             jax.ShapeDtypeStruct((rows, width), bf),
             jax.ShapeDtypeStruct((parent_rows, width), f32),
         ),
-        in_specs=[anyspace] * 4 + [vmem, smem, smem],
-        out_specs=(anyspace, anyspace),
+        in_specs=[hbm] * 4 + [vmem, smem, smem],
+        out_specs=(vmem, vmem),
         scratch_shapes=[
             pltpu.VMEM((rows, pivots), bf),
             pltpu.VMEM((under, pivots), bf),
@@ -401,7 +421,6 @@
             pltpu.VMEM((chunks, 2, 2, height, CHUNK), bf),
             pltpu.VMEM((parent_rows, 8 * slots * height), bf),
             pltpu.VMEM((parent_rows, width), bf),
-            pltpu.VMEM((chunks, parent_rows, CHUNK), f32),
             dma((2 * chunks, 4 * PER_LINK)),
             dma((2 * chunks, 4 * PER_LINK)),
             dma((chunks, 13)),
@@ -409,18 +428,29 @@
             dma((8,)),
             dma((8,)),
             dma((chunks + 3,)),
-            dma((2 * chunks,)),
         ],
         compiler_params=pltpu.CompilerParams(
-            collective_id=0, has_side_effects=True, vmem_limit_bytes=60 * 1024 * 1024
+            collective_id=0, has_side_effects=True, vmem_limit_bytes=48 * 1024 * 1024
         ),
         name="solve_extend_add",
     )(inv, below, rhs, parent_rhs, tile_rows, owners, tile_count)
+    return pl.pallas_call(
+        write_kernel,
+        out_shape=(
+            jax.ShapeDtypeStruct((rows, width), bf),
+            jax.ShapeDtypeStruct((parent_rows, width), f32),
+        ),
+        in_specs=[anyspace] * 2,
+        out_specs=(anyspace, anyspace),
+        scratch_shapes=[dma((2,))],
+        compiler_params=pltpu.CompilerParams(vmem_limit_bytes=1024 * 1024),
+        name="write",
+    )(solved, parent_new)
 
 
 def body(inv_diag, below, rhs, tile_count, tile_owner, tile_rows, parent_rhs):
     solved, parent_new = call(
-        inv_diag[0], below[0], rhs[0], parent_rhs[0], tile_rows[0], tile_owner[0, :, 0], tile_count
+        inv_diag[0], below[0], rhs[0], parent_rhs[0], tile_rows.transpose(1, 0, 2), tile_owner[0, :, 0], tile_count
     )
     return solved[None], parent_new[None]
 

time: 89.3 us -> 86.8 us (0.972)
  Pallas kernels: 83.6 us -> 82 us
  local copies, waits for them, and re-layouts: 4.81 us -> 3.89 us
    pallas_call x1, Pallas kernels: 83.6 us -> 81.1 us  [call(): pl.pallas_call(kernel, out_shape=(jax.ShapeDtypeStruct((rows, width), bf)...]
    unnamed x3 -> x10, local copies, waits for them, and re-layouts: 4.81 us -> 3.89 us
    pallas_call x0 -> x1, Pallas kernels: none -> 0.9 us  [call(): pl.pallas_call(write_kernel, out_shape=(jax.ShapeDtypeStruct((rows, width...]
where the time goes in v2:
time: 86.8 us; the launch traced here: 86.5 us
  Pallas kernels  82 us (94%)
  local copies, waits for them, and re-layouts  3.89 us (4%)
    pallas_call x1, Pallas kernels, call(): pl.pallas_call(kernel, out_shape=(jax.ShapeDtypeStruct((rows, width), bf)...  81.1 us
    unnamed x10, local copies, waits for them, and re-layouts  3.89 us

profile of v2, /device:TPU:1, one launch (start us, length us, event | category | flops | bytes accessed | tf_op | source)
XLA Modules:
  0.0 86.5 jit_solution(10920607484328639154)
XLA Ops:
  0.6 0.0 copy-start
  0.6 0.9 %copy-done = bf16[1,512,256]{2,1,0:T(8,128)(2,1)S(1)} copy-done((bf16[1,512,256]{2,1,0:T(8,128)(2,1)S(1)}, bf16[1,512,256]{2,1,0:T(8,128)(2,1)}, u32[]{:S(2)}) %copy-start) | copy-done | bytes 262168
  1.6 0.0 copy-start.1
  1.6 0.9 %copy-done.1 = bf16[1,512,256]{2,1,0:T(8,128)(2,1)S(1)} copy-done((bf16[1,512,256]{2,1,0:T(8,128)(2,1)S(1)}, bf16[1,512,256]{2,1,0:T(8,128)(2,1)}, u32[]{:S(2)}) %copy-start.1) | copy-done | bytes 262168
  2.5 0.0 copy-start.2
  2.5 0.7 copy-done.2
  3.2 0.0 copy-start.3
  3.2 0.7 copy-done.3
  3.9 0.0 copy-start.4
  3.9 0.7 copy-done.4
  4.5 81.1 %solve_extend_add.1 = (bf16[512,256]{1,0:T(8,128)(2,1)S(1)}, f32[512,256]{1,0:T(8,128)S(1)}) custom-call(bf16[512,8192]{1,0:T(8,128)(2,1)} %bitcast.13, bf16[768,8192]{1,0:T(8,128)(2,1)} %bitcast.12, bf16[512,256]{1,0:T(8,128)(2,1)S(1)} %bitcast.8, bf16[512,256]{1,0:T(8,128)(2,1)S(1)} %bitcast.9, s32[6,1,128]{2,1,0:T(1,128)S(1)} %bitcast.10, s32[6]{0:T(128)S(1)} %bitcast.11, ...), custom_call_target="tpu_custom_call" | custom-call | tf_op jit(solution)/shard_map/solve_extend_add/pallas_call | solution.py:400
  85.7 0.9 %write.1 = (bf16[512,256]{1,0:T(8,128)(2,1)}, f32[512,256]{1,0:T(8,128)}) custom-call(bf16[512,256]{1,0:T(8,128)(2,1)S(1)} %get-tuple-element.6.solved_in, f32[512,256]{1,0:T(8,128)S(1)} %get-tuple-element.7.parent_in), custom_call_target="tpu_custom_call" | custom-call | tf_op jit(solution)/shard_map/write/pallas_call | solution.py:437
Async XLA Ops:
  0.6 1.0 %copy-start = (bf16[1,512,256]{2,1,0:T(8,128)(2,1)S(1)}, bf16[1,512,256]{2,1,0:T(8,128)(2,1)}, u32[]{:S(2)}) copy-start(bf16[1,512,256]{2,1,0:T(8,128)(2,1)} %param.9) | copy-start | bytes 786436
  1.6 0.9 %copy-start.1 = (bf16[1,512,256]{2,1,0:T(8,128)(2,1)S(1)}, bf16[1,512,256]{2,1,0:T(8,128)(2,1)}, u32[]{:S(2)}) copy-start(bf16[1,512,256]{2,1,0:T(8,128)(2,1)} %param.13) | copy-start | bytes 786436
  2.5 0.7 copy-start.2
  3.2 0.7 copy-start.3
  3.9 0.7 copy-start.4

commit v3 on v2

--- a/solution.py
+++ b/solution.py
@@ -16,10 +16,10 @@
 
 
 def kernel(
-    inv_hbm, below_hbm, rhs_hbm, parent_hbm, rows_ref, owner_ref, count_ref,
+    inv_hbm, below_hbm, rhs_hbm, parent_hbm, rows_hbm, owner_hbm, count_hbm,
     solved_out, parent_out,
     inv, below, rbuf, sbuf, s_acc, u_acc, u_tiles, slot_idx,
-    rows_out, rows_in, packed, arrived, relayed, hits, parent,
+    rows_out, rows_in, packed, arrived, relayed, hits, parent, rows_ref, owner_ref, count_ref,
     g_send, g_recv, x_send, x_recv, r_send, r_recv, loc,
 ):
     f = lax.axis_index("front")
@@ -121,54 +121,65 @@
         for msg, j in ((R_OWN, 0), (R_NEAR_M, MINUS), (R_NEAR_P, PLUS), (R_OPP, 2)):
             g_r2(g, msg, j)
 
+    barrier = pltpu.get_barrier_semaphore()
+    for axis, s in DIRS:
+        pl.semaphore_signal(barrier, inc=1, device_id=(f, wide_of(vec(axis, s))), device_id_type=MESH)
+    for d in range(1, 8):
+        pl.semaphore_signal(barrier, inc=1, device_id=((f + d) % 8, w), device_id_type=MESH)
+
     own = pl.ds(pl.multiple_of(w * pb, pb), pb)
     loads = []
     for c in range(chunks):
         cols = pl.ds(c * CHUNK, CHUNK)
         loads.append(pltpu.make_async_copy(rhs_hbm.at[:, cols], rbuf.at[c, own], loc.at[c]))
+    smalls = [
+        pltpu.make_async_copy(rows_hbm, rows_ref, loc.at[chunks + 3]),
+        pltpu.make_async_copy(owner_hbm, owner_ref, loc.at[chunks + 4]),
+        pltpu.make_async_copy(count_hbm, count_ref, loc.at[chunks + 5]),
+    ]
     loads.append(pltpu.make_async_copy(inv_hbm, inv, loc.at[chunks]))
     loads.append(pltpu.make_async_copy(below_hbm, below, loc.at[chunks + 1]))
     loads.append(pltpu.make_async_copy(parent_hbm, parent, loc.at[chunks + 2]))
-    for copy in loads:
+    for copy in loads[:chunks] + smalls + loads[chunks:]:
         copy.start()
 
-    barrier = pltpu.get_barrier_semaphore()
-    for axis, s in DIRS:
-        pl.semaphore_signal(barrier, inc=1, device_id=(f, wide_of(vec(axis, s))), device_id_type=MESH)
-    for d in range(1, 8):
-        pl.semaphore_signal(barrier, inc=1, device_id=((f + d) % 8, w), device_id_type=MESH)
     pl.semaphore_wait(barrier, 11)
 
     loads[0].wait()
     g_own(0)
-
-    live = [w * tiles + j < count_ref[f] for j in range(tiles)]
-    none = jnp.full((1, height), parent_rows, jnp.int32)
-    rows_out[...] = jnp.full(rows_out.shape, parent_rows, jnp.int32)
-    for g in range(8):
-        index = [jnp.int32(0)] * slots
-        found = [jnp.int32(0)] * slots
-        seen = jnp.int32(0)
-        for j in range(tiles):
-            hit = owner_ref[j] == g
+    loads[1].wait()
+
+    def alive(j):
+        return w * tiles + j < count_ref[f]
+
+    def slots_of_tiles():
+        for copy in smalls:
+            copy.wait()
+        none = jnp.full((1, height), parent_rows, jnp.int32)
+        rows_out[...] = jnp.full(rows_out.shape, parent_rows, jnp.int32)
+        for g in range(8):
+            index = [jnp.int32(0)] * slots
+            found = [jnp.int32(0)] * slots
+            seen = jnp.int32(0)
+            for j in range(tiles):
+                hit = owner_ref[j] == g
+                for k in range(slots):
+                    this = jnp.logical_and(hit, seen == k)
+                    index[k] = jnp.where(this, j, index[k])
+                    found[k] = jnp.where(jnp.logical_and(this, alive(j)), 1, found[k])
+                seen = seen + jnp.where(hit, 1, 0)
             for k in range(slots):
-                this = jnp.logical_and(hit, seen == k)
-                index[k] = jnp.where(this, j, index[k])
-                found[k] = jnp.where(jnp.logical_and(this, live[j]), 1, found[k])
-            seen = seen + jnp.where(hit, 1, 0)
-        for k in range(slots):
-            slot_idx[g * slots + k] = index[k]
-            rows_out[g, k:k + 1, :] = jnp.where(found[k] == 1, rows_ref[index[k]], none)
-    rows_in[f] = rows_out[f]
-    rcopies = []
-    for d in range(1, 8):
-        to = (f + d) % 8
-        copy = pltpu.make_async_remote_copy(
-            src_ref=rows_out.at[to], dst_ref=rows_in.at[f], send_sem=r_send.at[d], recv_sem=r_recv.at[d],
-            device_id=(to, w), device_id_type=MESH,
-        )
-        copy.start()
-        sends.append(copy)
+                slot_idx[g * slots + k] = index[k]
+                rows_out[g, k:k + 1, :] = jnp.where(found[k] == 1, rows_ref[index[k]], none)
+        rows_in[f] = rows_out[f]
+        for d in range(1, 8):
+            to = (f + d) % 8
+            copy = pltpu.make_async_remote_copy(
+                src_ref=rows_out.at[to], dst_ref=rows_in.at[f], send_sem=r_send.at[d], recv_sem=r_recv.at[d],
+                device_id=(to, w), device_id_type=MESH,
+            )
+            copy.start()
+            sends.append(copy)
 
     def wait_rows():
         for d in range(1, 8):
@@ -217,7 +228,7 @@
     def pack(c):
         for j in range(tiles):
             value = u_acc[j * height:(j + 1) * height, :]
-            u_tiles[j] = jnp.where(live[j], value, jnp.zeros_like(value)).astype(jnp.bfloat16)
+            u_tiles[j] = jnp.where(alive(j), value, jnp.zeros_like(value)).astype(jnp.bfloat16)
 
         def one(i, carry):
             for k in range(slots):
@@ -284,8 +295,8 @@
     def at_far(i):
         return wide_of((2 * i, 2 - 2 * i))
 
-    def at_farther(i):
-        return wide_of((2 * (1 - i // 2) + sign(i) * (i // 2), sign(i) * (1 - i // 2) + 2 * (i // 2)))
+    def at_farther(i, j):
+        return wide_of((2 * (1 - i) + j * i, j * (1 - i) + 2 * i))
 
     sides = [(inv, s_acc)] * chunks + [(below, u_acc)] * chunks
 
@@ -297,20 +308,15 @@
         acc[...] = jnp.zeros_like(acc)
         take(g, 1, lambda i: w)
 
-    def middle(g):
-        take_own(g)
-        g_d2own(g)
-        take(g, 4, at_near)
-        g_d2near(g)
-
     def late_first(g):
         g_r2(g, R_OWN, 0)
         take(g, 2, at_far)
 
     def late_last(g):
         g_r2(g, R_NEAR_M, MINUS)
+        take(g, 2, lambda i: at_farther(i, MINUS))
         g_r2(g, R_NEAR_P, PLUS)
-        take(g, 4, at_farther)
+        take(g, 2, lambda i: at_farther(i, PLUS))
         g_r2(g, R_OPP, 2)
         take(g, 1, lambda i: wide_of((2, 2)))
 
@@ -319,42 +325,54 @@
         sbuf[c, own, :] = value
         solved_out[:, c * CHUNK:(c + 1) * CHUNK] = value
 
+    g_own(1)
+    slots_of_tiles()
     g_d1(0)
     g_r1(0)
-    loads[1].wait()
     loads[2].wait()
-    middle(0)
-    g_own(1)
+    take_own(0)
+    g_d2own(0)
+    take(0, 4, at_near)
+    g_d2near(0)
+    g_d1(1)
     take(0, 4, at_diagonal)
     g_d2opp(0)
     wait_rows()
     build_hits()
-    g_d1(1)
+    g_r1(1)
     late_first(0)
-    g_r1(1)
+    g_d2own(1)
     late_last(0)
     store_solved(0)
-    middle(1)
     g_own(2)
+    take_own(1)
+    take(1, 4, at_near)
+    g_d2near(1)
+    g_d1(2)
     take(1, 4, at_diagonal)
     g_d2opp(1)
-    g_d1(2)
+    g_r1(2)
     late_first(1)
-    g_r1(2)
+    g_d2own(2)
     late_last(1)
     store_solved(1)
+    g_own(3)
     loads[3].wait()
-    middle(2)
-    g_own(3)
+    take_own(2)
+    take(2, 4, at_near)
+    g_d2near(2)
+    g_d1(3)
     take(2, 4, at_diagonal)
     g_d2opp(2)
-    g_d1(3)
+    g_r1(3)
     late_first(2)
-    g_r1(3)
+    g_d2own(3)
     late_last(2)
     pack(0)
     xsend(0)
-    middle(3)
+    take_own(3)
+    take(3, 4, at_near)
+    g_d2near(3)
     xrelay(0)
     take(3, 4, at_diagonal)
     g_d2opp(3)
@@ -395,15 +413,14 @@
     anyspace = pl.BlockSpec(memory_space=pl.ANY)
     hbm = pl.BlockSpec(memory_space=pltpu.HBM)
     vmem = pl.BlockSpec(memory_space=pltpu.VMEM)
-    smem = pl.BlockSpec(memory_space=pltpu.SMEM)
     dma = pltpu.SemaphoreType.DMA
     solved, parent_new = pl.pallas_call(
         kernel,
         out_shape=(
-            jax.ShapeDtypeStruct((rows, width), bf),
-            jax.ShapeDtypeStruct((parent_rows, width), f32),
+            pltpu.VMEM((rows, width), bf),
+            pltpu.VMEM((parent_rows, width), f32),
         ),
-        in_specs=[hbm] * 4 + [vmem, smem, smem],
+        in_specs=[hbm] * 7,
         out_specs=(vmem, vmem),
         scratch_shapes=[
             pltpu.VMEM((rows, pivots), bf),
@@ -421,16 +438,19 @@
             pltpu.VMEM((chunks, 2, 2, height, CHUNK), bf),
             pltpu.VMEM((parent_rows, 8 * slots * height), bf),
             pltpu.VMEM((parent_rows, width), bf),
+            pltpu.VMEM(tile_rows.shape, jnp.int32),
+            pltpu.SMEM(owners.shape, jnp.int32),
+            pltpu.SMEM(tile_count.shape, jnp.int32),
             dma((2 * chunks, 4 * PER_LINK)),
             dma((2 * chunks, 4 * PER_LINK)),
             dma((chunks, 13)),
             dma((chunks, 13)),
             dma((8,)),
             dma((8,)),
-            dma((chunks + 3,)),
+            dma((chunks + 6,)),
         ],
         compiler_params=pltpu.CompilerParams(
-            collective_id=0, has_side_effects=True, vmem_limit_bytes=48 * 1024 * 1024
+            collective_id=0, has_side_effects=True, vmem_limit_bytes=60 * 1024 * 1024
         ),
         name="solve_extend_add",
     )(inv, below, rhs, parent_rhs, tile_rows, owners, tile_count)

time: 86.8 us -> 78.2 us (0.901)
  Pallas kernels: 82 us -> 77.5 us
  local copies, waits for them, and re-layouts: 3.89 us -> 0 us
    pallas_call x1, Pallas kernels: 81.1 us -> 76.6 us  [call(): pl.pallas_call(kernel, out_shape=(pltpu.VMEM((rows, width), bf), pltpu.VM...]
    unnamed x10 -> x0, local copies, waits for them, and re-layouts: 3.89 us -> none
where the time goes in v3:
time: 78.2 us; the launch traced here: 78.1 us
  Pallas kernels  77.5 us (99%)
    pallas_call x1, Pallas kernels, call(): pl.pallas_call(kernel, out_shape=(pltpu.VMEM((rows, width), bf), pltpu.VM...  76.6 us

profile of v3, /device:TPU:1, one launch (start us, length us, event | category | flops | bytes accessed | tf_op | source)
XLA Modules:
  0.0 78.1 jit_solution(2125451013784931724)
XLA Ops:
  0.6 76.6 %solve_extend_add.1 = (bf16[512,256]{1,0:T(8,128)(2,1)S(1)}, f32[512,256]{1,0:T(8,128)S(1)}) custom-call(bf16[512,8192]{1,0:T(8,128)(2,1)} %bitcast.9, bf16[768,8192]{1,0:T(8,128)(2,1)} %bitcast.8, bf16[512,256]{1,0:T(8,128)(2,1)} %bitcast.10, bf16[512,256]{1,0:T(8,128)(2,1)} %bitcast.11, s32[6,1,128]{2,1,0:T(1,128)} %bitcast.12, s32[6]{0:T(128)} %bitcast.13, ...), custom_call_target="tpu_custom_call" | custom-call | tf_op jit(solution)/shard_map/solve_extend_add/pallas_call | solution.py:417
  77.2 0.9 %write.1 = (bf16[512,256]{1,0:T(8,128)(2,1)}, f32[512,256]{1,0:T(8,128)}) custom-call(bf16[512,256]{1,0:T(8,128)(2,1)S(1)} %get-tuple-element.6.solved_in, f32[512,256]{1,0:T(8,128)S(1)} %get-tuple-element.7.parent_in), custom_call_target="tpu_custom_call" | custom-call | tf_op jit(solution)/shard_map/write/pallas_call | solution.py:457

commit v4 on v3

--- a/solution.py
+++ b/solution.py
@@ -19,7 +19,7 @@
     inv_hbm, below_hbm, rhs_hbm, parent_hbm, rows_hbm, owner_hbm, count_hbm,
     solved_out, parent_out,
     inv, below, rbuf, sbuf, s_acc, u_acc, u_tiles, slot_idx,
-    rows_out, rows_in, packed, arrived, relayed, hits, parent, rows_ref, owner_ref, count_ref,
+    rows_out, rows_in, packed, arrived, hits, parent, rows_ref, owner_ref, count_ref,
     g_send, g_recv, x_send, x_recv, r_send, r_recv, loc,
 ):
     f = lax.axis_index("front")
@@ -76,12 +76,16 @@
             gsend(g, axis, s, OWN, region(g, here, 1 - axis))
 
     def g_d1(g):
+        def near(axis, s):
+            for t in (PLUS, MINUS):
+                gsend(g, 1 - axis, t, NEAR_M if s == PLUS else NEAR_P, region(g, vec(axis, -s), axis))
+
         for axis, s in DIRS:
             off = vec(axis, -s)
             gwait(g, axis, s, D1, region(g, off, axis))
             gsend(g, axis, s, R1, region(g, off, axis, quart(s)))
-            for t in (PLUS, MINUS):
-                gsend(g, 1 - axis, t, NEAR_M if s == PLUS else NEAR_P, region(g, off, axis))
+        for axis, s in DIRS:
+            near(axis, s)
 
     def g_r1(g):
         for axis, s in DIRS:
@@ -148,6 +152,7 @@
     loads[0].wait()
     g_own(0)
     loads[1].wait()
+    g_own(1)
 
     def alive(j):
         return w * tiles + j < count_ref[f]
@@ -230,58 +235,42 @@
             value = u_acc[j * height:(j + 1) * height, :]
             u_tiles[j] = jnp.where(alive(j), value, jnp.zeros_like(value)).astype(jnp.bfloat16)
 
-        def one(i, carry):
-            for k in range(slots):
-                packed[c, i, k] = u_tiles[slot_idx[i * slots + k]]
-            return carry
-
-        lax.fori_loop(0, 8, one, 0)
+    def pack_for(c, to):
         for k in range(slots):
-            arrived[c, f, k] = packed[c, f, k]
+            packed[c, to, k] = u_tiles[slot_idx[to * slots + k]]
 
     def xsend(c):
-        for n, s in enumerate((PLUS, MINUS)):
-            for c2 in range(2):
-                to = chip_at(2) * 2 + c2
-                xstart(c, 5 + n * 2 + c2, 5 + n * 2 + c2, packed.at[c, to, n], relayed.at[c, n, c2], chip_at(s) * 2 + core)
+        for c2 in range(2):
+            to = chip_at(2) * 2 + c2
+            pack_for(c, to)
+            xstart(c, 5 + c2, 5 + core, packed.at[c, to], arrived.at[c, f], to)
         for n, s in enumerate((PLUS, MINUS)):
             for c2 in range(2):
                 to = chip_at(s) * 2 + c2
+                pack_for(c, to)
                 xstart(c, 1 + n * 2 + c2, 1 + n * 2 + core, packed.at[c, to], arrived.at[c, f], to)
         to = chip * 2 + 1 - core
+        pack_for(c, to)
         xstart(c, 0, 0, packed.at[c, to], arrived.at[c, f], to)
-
-    def xrelay(c):
-        for n, s in enumerate((PLUS, MINUS)):
+        for k in range(slots):
+            arrived[c, f, k] = u_tiles[slot_idx[f * slots + k]]
+
+    def add_chip(c, k):
+        other = chip * 2 + 1 - core
+        if k == 0:
+            ref = arrived.at[c, other]
+            xcopy(c, 0, 0, ref, ref, other).wait_recv()
+        else:
+            first = {-1: 1, 1: 3, 2: 5}[k]
             for c2 in range(2):
-                ref = relayed.at[c, n, c2]
-                xcopy(c, 5 + n * 2 + c2, 5 + n * 2 + c2, ref, ref, chip_at(s) * 2 + core).wait_recv()
-                source = chip_at(-s) * 2 + core
-                xstart(c, 9 + n * 2 + c2, 9 + n * 2 + core, ref, arrived.at[c, source, n], chip_at(s) * 2 + c2)
-
-    def xwait(c):
-        other = chip * 2 + 1 - core
-        ref = arrived.at[c, other]
-        xcopy(c, 0, 0, ref, ref, other).wait_recv()
-        for n, s in enumerate((PLUS, MINUS)):
-            for c2 in range(2):
-                ref = arrived.at[c, chip_at(-s) * 2 + c2]
-                xcopy(c, 0, 1 + n * 2 + c2, ref, ref, other).wait_recv()
-        for n, s in enumerate((PLUS, MINUS)):
-            for c2 in range(2):
-                ref = arrived.at[c, chip_at(2) * 2 + c2, n]
-                xcopy(c, 0, 9 + n * 2 + c2, ref, ref, other).wait_recv()
-
-    def scatter(c):
+                ref = arrived.at[c, chip_at(k) * 2 + c2]
+                xcopy(c, 0, first + c2, ref, ref, other).wait_recv()
         cols = slice(c * CHUNK, (c + 1) * CHUNK)
-        per = 4 * slots * height
-
-        def step(i, acc):
-            at = pl.ds(pl.multiple_of(i * per, per), per)
-            values = arrived[c, pl.ds(i * 4, 4)].reshape(per, CHUNK)
-            return acc - jnp.dot(hits[:, at], values, preferred_element_type=jnp.float32)
-
-        parent_out[:, cols] = step(1, step(0, parent[:, cols].astype(jnp.float32)))
+        per = 2 * slots * height
+        values = arrived[c, pl.ds(chip_at(k) * 2, 2)].reshape(per, CHUNK)
+        at = pl.ds(pl.multiple_of(chip_at(k) * per, per), per)
+        before = parent[:, cols].astype(jnp.float32) if k == 0 else parent_out[:, cols]
+        parent_out[:, cols] = before - jnp.dot(hits[:, at], values, preferred_element_type=jnp.float32)
 
     def sign(i):
         return 2 * (i % 2) - 1
@@ -325,7 +314,6 @@
         sbuf[c, own, :] = value
         solved_out[:, c * CHUNK:(c + 1) * CHUNK] = value
 
-    g_own(1)
     slots_of_tiles()
     g_d1(0)
     g_r1(0)
@@ -373,7 +361,6 @@
     take_own(3)
     take(3, 4, at_near)
     g_d2near(3)
-    xrelay(0)
     take(3, 4, at_diagonal)
     g_d2opp(3)
     late_first(3)
@@ -381,11 +368,10 @@
     pack(1)
     xsend(1)
     loads[4].wait()
-    xwait(0)
-    scatter(0)
-    xrelay(1)
-    xwait(1)
-    scatter(1)
+    for k in (0, -1, 1, 2):
+        add_chip(0, k)
+    for k in (0, -1, 1, 2):
+        add_chip(1, k)
     for copy in sends:
         copy.wait_send()
 
@@ -435,7 +421,6 @@
             pltpu.VMEM((8, 8, height), jnp.int32),
             pltpu.VMEM((chunks, 8, slots, height, CHUNK), bf),
             pltpu.VMEM((chunks, 8, slots, height, CHUNK), bf),
-            pltpu.VMEM((chunks, 2, 2, height, CHUNK), bf),
             pltpu.VMEM((parent_rows, 8 * slots * height), bf),
             pltpu.VMEM((parent_rows, width), bf),
             pltpu.VMEM(tile_rows.shape, jnp.int32),
@@ -443,8 +428,8 @@
             pltpu.SMEM(tile_count.shape, jnp.int32),
             dma((2 * chunks, 4 * PER_LINK)),
             dma((2 * chunks, 4 * PER_LINK)),
-            dma((chunks, 13)),
-            dma((chunks, 13)),
+            dma((chunks, 7)),
+            dma((chunks, 7)),
             dma((8,)),
             dma((8,)),
             dma((chunks + 6,)),

time: 78.2 us -> 70.6 us (0.903)
  Pallas kernels: 77.5 us -> 69.8 us
    pallas_call x1, Pallas kernels: 76.6 us -> 68.9 us  [call(): pl.pallas_call(kernel, out_shape=(pltpu.VMEM((rows, width), bf), pltpu.VM...]
where the time goes in v4:
time: 70.6 us; the launch traced here: 70.5 us
  Pallas kernels  69.8 us (99%)
    pallas_call x1, Pallas kernels, call(): pl.pallas_call(kernel, out_shape=(pltpu.VMEM((rows, width), bf), pltpu.VM...  68.9 us

profile of v4, /device:TPU:1, one launch (start us, length us, event | category | flops | bytes accessed | tf_op | source)
XLA Modules:
  0.0 70.5 jit_solution(14035841315999108459)
XLA Ops:
  0.6 68.9 %solve_extend_add.1 = (bf16[512,256]{1,0:T(8,128)(2,1)S(1)}, f32[512,256]{1,0:T(8,128)S(1)}) custom-call(bf16[512,8192]{1,0:T(8,128)(2,1)} %bitcast.9, bf16[768,8192]{1,0:T(8,128)(2,1)} %bitcast.8, bf16[512,256]{1,0:T(8,128)(2,1)} %bitcast.10, bf16[512,256]{1,0:T(8,128)(2,1)} %bitcast.11, s32[6,1,128]{2,1,0:T(1,128)} %bitcast.12, s32[6]{0:T(128)} %bitcast.13, ...), custom_call_target="tpu_custom_call" | custom-call | tf_op jit(solution)/shard_map/solve_extend_add/pallas_call | solution.py:403
  69.6 0.9 %write.1 = (bf16[512,256]{1,0:T(8,128)(2,1)}, f32[512,256]{1,0:T(8,128)}) custom-call(bf16[512,256]{1,0:T(8,128)(2,1)S(1)} %get-tuple-element.6.solved_in, f32[512,256]{1,0:T(8,128)S(1)} %get-tuple-element.7.parent_in), custom_call_target="tpu_custom_call" | custom-call | tf_op jit(solution)/shard_map/write/pallas_call | solution.py:442

commit v5 on v4

--- a/solution.py
+++ b/solution.py
@@ -347,22 +347,22 @@
     g_own(3)
     loads[3].wait()
     take_own(2)
+    g_d2near(2)
     take(2, 4, at_near)
-    g_d2near(2)
+    g_d2opp(2)
     g_d1(3)
     take(2, 4, at_diagonal)
-    g_d2opp(2)
+    late_first(2)
     g_r1(3)
-    late_first(2)
     g_d2own(3)
     late_last(2)
     pack(0)
     xsend(0)
+    g_d2near(3)
     take_own(3)
     take(3, 4, at_near)
-    g_d2near(3)
+    g_d2opp(3)
     take(3, 4, at_diagonal)
-    g_d2opp(3)
     late_first(3)
     late_last(3)
     pack(1)

time: 70.6 us -> 69 us (0.977)
  Pallas kernels: 69.8 us -> 68.2 us
    pallas_call x1, Pallas kernels: 68.9 us -> 67.3 us  [call(): pl.pallas_call(kernel, out_shape=(pltpu.VMEM((rows, width), bf), pltpu.VM...]
where the time goes in v5:
time: 69 us; the launch traced here: 68.9 us
  Pallas kernels  68.2 us (99%)
    pallas_call x1, Pallas kernels, call(): pl.pallas_call(kernel, out_shape=(pltpu.VMEM((rows, width), bf), pltpu.VM...  67.3 us

profile of v5, /device:TPU:1, one launch (start us, length us, event | category | flops | bytes accessed | tf_op | source)
XLA Modules:
  0.0 68.9 jit_solution(7768219624048651061)
XLA Ops:
  0.6 67.3 %solve_extend_add.1 = (bf16[512,256]{1,0:T(8,128)(2,1)S(1)}, f32[512,256]{1,0:T(8,128)S(1)}) custom-call(bf16[512,8192]{1,0:T(8,128)(2,1)} %bitcast.9, bf16[768,8192]{1,0:T(8,128)(2,1)} %bitcast.8, bf16[512,256]{1,0:T(8,128)(2,1)} %bitcast.10, bf16[512,256]{1,0:T(8,128)(2,1)} %bitcast.11, s32[6,1,128]{2,1,0:T(1,128)} %bitcast.12, s32[6]{0:T(128)} %bitcast.13, ...), custom_call_target="tpu_custom_call" | custom-call | tf_op jit(solution)/shard_map/solve_extend_add/pallas_call | solution.py:403
  68.0 0.9 %write.1 = (bf16[512,256]{1,0:T(8,128)(2,1)}, f32[512,256]{1,0:T(8,128)}) custom-call(bf16[512,256]{1,0:T(8,128)(2,1)S(1)} %get-tuple-element.6.solved_in, f32[512,256]{1,0:T(8,128)S(1)} %get-tuple-element.7.parent_in), custom_call_target="tpu_custom_call" | custom-call | tf_op jit(solution)/shard_map/write/pallas_call | solution.py:442

commit v6 on v5

--- a/solution.py
+++ b/solution.py
@@ -240,20 +240,18 @@
             packed[c, to, k] = u_tiles[slot_idx[to * slots + k]]
 
     def xsend(c):
-        for c2 in range(2):
-            to = chip_at(2) * 2 + c2
-            pack_for(c, to)
-            xstart(c, 5 + c2, 5 + core, packed.at[c, to], arrived.at[c, f], to)
+        steps = [(chip_at(2) * 2 + c2, 5 + c2, 5 + core) for c2 in range(2)]
         for n, s in enumerate((PLUS, MINUS)):
-            for c2 in range(2):
-                to = chip_at(s) * 2 + c2
-                pack_for(c, to)
-                xstart(c, 1 + n * 2 + c2, 1 + n * 2 + core, packed.at[c, to], arrived.at[c, f], to)
-        to = chip * 2 + 1 - core
-        pack_for(c, to)
-        xstart(c, 0, 0, packed.at[c, to], arrived.at[c, f], to)
-        for k in range(slots):
-            arrived[c, f, k] = u_tiles[slot_idx[f * slots + k]]
+            steps += [(chip_at(s) * 2 + c2, 1 + n * 2 + c2, 1 + n * 2 + core) for c2 in range(2)]
+        steps.append((chip * 2 + 1 - core, 0, 0))
+        pack_for(c, steps[0][0])
+        for i, (to, sid, rid) in enumerate(steps):
+            if i + 1 < len(steps):
+                pack_for(c, steps[i + 1][0])
+            else:
+                for k in range(slots):
+                    arrived[c, f, k] = u_tiles[slot_idx[f * slots + k]]
+            xstart(c, sid, rid, packed.at[c, to], arrived.at[c, f], to)
 
     def add_chip(c, k):
         other = chip * 2 + 1 - core
@@ -332,8 +330,8 @@
     g_d2own(1)
     late_last(0)
     store_solved(0)
+    take_own(1)
     g_own(2)
-    take_own(1)
     take(1, 4, at_near)
     g_d2near(1)
     g_d1(2)
@@ -344,9 +342,9 @@
     g_d2own(2)
     late_last(1)
     store_solved(1)
-    g_own(3)
     loads[3].wait()
     take_own(2)
+    g_own(3)
     g_d2near(2)
     take(2, 4, at_near)
     g_d2opp(2)

time: 69 us -> 69.3 us (level)
  no operation moved by 1% of the time
where the time goes in v6:
time: 69.3 us; the launch traced here: 69.2 us
  Pallas kernels  68.5 us (99%)
    pallas_call x1, Pallas kernels, call(): pl.pallas_call(kernel, out_shape=(pltpu.VMEM((rows, width), bf), pltpu.VM...  67.6 us

profile of v6, /device:TPU:1, one launch (start us, length us, event | category | flops | bytes accessed | tf_op | source)
XLA Modules:
  0.0 69.2 jit_solution(10395137492701472950)
XLA Ops:
  0.6 67.6 %solve_extend_add.1 = (bf16[512,256]{1,0:T(8,128)(2,1)S(1)}, f32[512,256]{1,0:T(8,128)S(1)}) custom-call(bf16[512,8192]{1,0:T(8,128)(2,1)} %bitcast.9, bf16[768,8192]{1,0:T(8,128)(2,1)} %bitcast.8, bf16[512,256]{1,0:T(8,128)(2,1)} %bitcast.10, bf16[512,256]{1,0:T(8,128)(2,1)} %bitcast.11, s32[6,1,128]{2,1,0:T(1,128)} %bitcast.12, s32[6]{0:T(128)} %bitcast.13, ...), custom_call_target="tpu_custom_call" | custom-call | tf_op jit(solution)/shard_map/solve_extend_add/pallas_call | solution.py:401
  68.3 0.9 %write.1 = (bf16[512,256]{1,0:T(8,128)(2,1)}, f32[512,256]{1,0:T(8,128)}) custom-call(bf16[512,256]{1,0:T(8,128)(2,1)S(1)} %get-tuple-element.6.solved_in, f32[512,256]{1,0:T(8,128)S(1)} %get-tuple-element.7.parent_in), custom_call_target="tpu_custom_call" | custom-call | tf_op jit(solution)/shard_map/write/pallas_call | solution.py:440
